TPU v7x, 32 devices: a whole 2x2x4 slice. The times are simulated.
32 devices in a mesh: shard: 8 (over y, x, core), replica: 4 (over z).
Axes of the slice: x: 2, y: 2, z: 4, core: 2. Of those that a mesh axis runs over, the one named last changes fastest.
Arguments:
- hidden: bfloat16 [8192, 768], P(('replica', 'shard')), may hold values from -6 to 6
- segment_ids: int32 [8192], P(('replica', 'shard')), may hold values from 0 to 63, as said below
- w_qkv: bfloat16 [768, 2304], P('shard'), may hold values from -0.21875 to 0.21875
- b_qv: bfloat16 [2, 768], P(None, 'shard'), may hold values from -3 to 3
- w_out: bfloat16 [768, 768], P('shard'), may hold values from -3 to 3
- b_out: bfloat16 [768], P('shard'), may hold values from -3 to 3
- gain1: bfloat16 [768], P('shard'), may hold values from 0.5 to 1.5
- shift1: bfloat16 [768], P('shard'), may hold values from -3 to 3
- w_in: bfloat16 [768, 3072], P('shard'), may hold values from -0.21875 to 0.21875
- b_in: bfloat16 [3072], P('shard'), may hold values from -3 to 3
- w_back: bfloat16 [3072, 768], P('shard'), may hold values from -0.21875 to 0.21875
- b_back: bfloat16 [768], P('shard'), may hold values from -3 to 3
- gain2: bfloat16 [768], P('shard'), may hold values from 0.5 to 1.5
- shift2: bfloat16 [768], P('shard'), may hold values from -3 to 3
- cotangent: float32 [8192, 768], P(('replica', 'shard')), may hold values from -6 to 6
Outputs:
- output: bfloat16 [8192, 768], P(('replica', 'shard'))
- d_hidden: float32 [8192, 768], P(('replica', 'shard'))
- grad_w_qkv: float32 [768, 2304], P('shard')
- grad_b_qv: float32 [2, 768], P(None, 'shard')
- grad_w_out: float32 [768, 768], P('shard')
- grad_b_out: float32 [768], P('shard')
- grad_gain1: float32 [768], P('shard')
- grad_shift1: float32 [768], P('shard')
- grad_w_in: float32 [768, 3072], P('shard')
- grad_b_in: float32 [3072], P('shard')
- grad_w_back: float32 [3072, 768], P('shard')
- grad_b_back: float32 [768], P('shard')
- grad_gain2: float32 [768], P('shard')
- grad_shift2: float32 [768], P('shard')
Inputs may be any that keep to these rules, and one draw needn't show every extreme that they name: `segment_ids`: ids never fall along the tokens. Sequence s (tokens s * 2048 to (s + 1) * 2048 - 1) holds exactly 16 documents with ids s * 16 to s * 16 + 15, one of them 1280 tokens long.
All inputs are finite; a program needn't handle non-finite values.
Results may differ from a plain program's by a relative error of at most 0.023.
Values may be sent and summed in bfloat16 or wider, within the bound.
A program may use at most 192 MiB of HBM per device.

v0:
```python
import math
import jax
import jax.numpy as jnp
from jax import lax
from jax.sharding import PartitionSpec as P

HEADS = 12
scale_factor = 0.125
norm_epsilon = 1e-05
masked_value = -1e30


def normalize(resid, gain, shift):
    mean_value = jnp.mean(resid, axis=-1, keepdims=True)
    centered = resid - mean_value
    variance = jnp.mean(centered * centered, axis=-1, keepdims=True)
    return centered * lax.rsqrt(variance + norm_epsilon) * gain + shift


def gelu_exact(values):
    return jax.nn.gelu(values, approximate=False)


def keep_state(state):
    return state


def block_size(count):
    return math.gcd(count, 512)


def masked_scores(query_heads, key_heads, query_segs, key_segs):
    scores = (
        jnp.einsum("qhd,khd->hqk", query_heads, key_heads, preferred_element_type=jnp.float32)
        * scale_factor
    )
    allowed = query_segs[:, None] == key_segs[None, :]
    return (scores, allowed[None])


def grad_block(
    query_heads, dctx_heads, log_total, delta, query_segs, key_heads, value_heads, key_segs
):
    scores, allowed = masked_scores(query_heads, key_heads, query_segs, key_segs)
    probs = jnp.where(allowed, jnp.exp(scores - log_total[:, :, None]), 0.0)
    d_prob = jnp.einsum("qhd,khd->hqk", dctx_heads, value_heads, preferred_element_type=jnp.float32)
    d_scores = (probs * (d_prob - delta[:, :, None])).astype(jnp.bfloat16)
    return (probs.astype(jnp.bfloat16), d_scores)


def body(
    hidden,
    segment_ids,
    w_qkv,
    b_qv,
    w_out,
    b_out,
    gain1,
    shift1,
    w_in,
    b_in,
    w_back,
    b_back,
    gain2,
    shift2,
    cotangent,
):
    tok_rows, width = hidden.shape
    heads = HEADS
    head_dim = width // heads
    seg_low = segment_ids[0]
    seg_high = segment_ids[-1]
    wq_full, wo_full, bqv_full, bo_full, g1_full, s1_full = (
        lax.all_gather(w_qkv, "shard", axis=0, tiled=True),
        lax.all_gather(w_out, "shard", axis=0, tiled=True),
        lax.all_gather(b_qv, "shard", axis=1, tiled=True),
        lax.all_gather(b_out, "shard", axis=0, tiled=True),
        lax.all_gather(gain1, "shard", axis=0, tiled=True),
        lax.all_gather(shift1, "shard", axis=0, tiled=True),
    )
    qkv = jnp.dot(hidden, wq_full, preferred_element_type=jnp.float32)
    bqv_wide = bqv_full.astype(jnp.float32)
    query = (qkv[:, :width] + bqv_wide[0]).astype(jnp.bfloat16)
    keys = qkv[:, width : 2 * width].astype(jnp.bfloat16)
    values = (qkv[:, 2 * width :] + bqv_wide[1]).astype(jnp.bfloat16)
    query_heads = query.reshape(tok_rows, heads, head_dim)
    key_local = keys.reshape(tok_rows, heads, head_dim)
    value_local = values.reshape(tok_rows, heads, head_dim)
    start_state = (
        jnp.full((heads, tok_rows), masked_value, jnp.float32),
        jnp.zeros((heads, tok_rows), jnp.float32),
        jnp.zeros((tok_rows, heads, head_dim), jnp.float32),
    )
    key_piece = lax.all_gather(keys, "shard", axis=0, tiled=True)
    value_piece = lax.all_gather(values, "shard", axis=0, tiled=True)
    seg_piece = lax.all_gather(segment_ids, "shard", axis=0, tiled=True)
    count = key_piece.shape[0]
    block = block_size(count)

    def forward_step(index, state):
        offset = index * block
        key_heads = lax.dynamic_slice_in_dim(key_piece, offset, block, 0).reshape(
            block, heads, head_dim
        )
        value_heads = lax.dynamic_slice_in_dim(value_piece, offset, block, 0).reshape(
            block, heads, head_dim
        )
        key_segs = lax.dynamic_slice_in_dim(seg_piece, offset, block, 0)

        def forward_update(state):
            running_max, running_sum, accum = state
            scores, allowed = masked_scores(query_heads, key_heads, segment_ids, key_segs)
            new_max = jnp.maximum(
                running_max, jnp.max(jnp.where(allowed, scores, masked_value), axis=-1)
            )
            factor = jnp.exp(running_max - new_max)
            weights = jnp.where(allowed, jnp.exp(scores - new_max[:, :, None]), 0.0)
            running_sum = running_sum * factor + jnp.sum(weights, axis=-1)
            accum = accum * factor.T[:, :, None] + jnp.einsum(
                "hqk,khd->qhd",
                weights.astype(jnp.bfloat16),
                value_heads,
                preferred_element_type=jnp.float32,
            )
            return (new_max, running_sum, accum)

        touches = jnp.logical_and(key_segs[0] <= seg_high, key_segs[-1] >= seg_low)
        return lax.cond(touches, forward_update, keep_state, state)

    running_max, running_sum, accum = lax.fori_loop(0, count // block, forward_step, start_state)
    context32 = accum / running_sum.T[:, :, None]
    log_total = running_max + jnp.log(running_sum)
    context = context32.reshape(tok_rows, width).astype(jnp.bfloat16)
    resid1 = (
        hidden.astype(jnp.float32)
        + jnp.dot(context, wo_full, preferred_element_type=jnp.float32)
        + bo_full.astype(jnp.float32)
    )
    normed1, norm1_pull = jax.vjp(
        normalize, resid1, g1_full.astype(jnp.float32), s1_full.astype(jnp.float32)
    )
    wi_full, bi_full, wb_full, bb_full, g2_full, s2_full = (
        lax.all_gather(w_in, "shard", axis=0, tiled=True),
        lax.all_gather(b_in, "shard", axis=0, tiled=True),
        lax.all_gather(w_back, "shard", axis=0, tiled=True),
        lax.all_gather(b_back, "shard", axis=0, tiled=True),
        lax.all_gather(gain2, "shard", axis=0, tiled=True),
        lax.all_gather(shift2, "shard", axis=0, tiled=True),
    )
    normed1_low = normed1.astype(jnp.bfloat16)
    pre = jnp.dot(normed1_low, wi_full, preferred_element_type=jnp.float32) + bi_full.astype(
        jnp.float32
    )
    act, gelu_pull = jax.vjp(gelu_exact, pre)
    act_low = act.astype(jnp.bfloat16)
    resid2 = (
        normed1
        + jnp.dot(act_low, wb_full, preferred_element_type=jnp.float32)
        + bb_full.astype(jnp.float32)
    )
    out32, norm2_pull = jax.vjp(
        normalize, resid2, g2_full.astype(jnp.float32), s2_full.astype(jnp.float32)
    )
    output = out32.astype(jnp.bfloat16)
    d_resid2, grad_gain2, grad_shift2 = norm2_pull(cotangent)
    d_branch2 = d_resid2.astype(jnp.bfloat16)
    grad_b_back = jnp.sum(d_resid2, axis=0)
    grad_w_back = jnp.einsum("tf,td->fd", act_low, d_branch2, preferred_element_type=jnp.float32)
    d_act = jnp.einsum("td,fd->tf", d_branch2, wb_full, preferred_element_type=jnp.float32)
    (d_pre,) = gelu_pull(d_act)
    grad_b_in = jnp.sum(d_pre, axis=0)
    d_pre_low = d_pre.astype(jnp.bfloat16)
    grad_w_in = jnp.einsum("td,tf->df", normed1_low, d_pre_low, preferred_element_type=jnp.float32)
    d_normed1 = d_resid2 + jnp.einsum(
        "tf,df->td", d_pre_low, wi_full, preferred_element_type=jnp.float32
    )
    d_resid1, grad_gain1, grad_shift1 = norm1_pull(d_normed1)
    grad_b_out = jnp.sum(d_resid1, axis=0)
    d_branch1 = d_resid1.astype(jnp.bfloat16)
    grad_w_out = jnp.einsum("tc,td->cd", context, d_branch1, preferred_element_type=jnp.float32)
    d_context = jnp.einsum(
        "td,cd->tc", d_branch1, wo_full, preferred_element_type=jnp.float32
    ).astype(jnp.bfloat16)
    dctx_heads = d_context.reshape(tok_rows, heads, head_dim)
    delta = jnp.einsum("qhd,qhd->hq", dctx_heads.astype(jnp.float32), context32)
    zero_heads = jnp.zeros((tok_rows, heads, head_dim), jnp.float32)
    query_key_piece = lax.all_gather(keys, "shard", axis=0, tiled=True)
    query_value_piece = lax.all_gather(values, "shard", axis=0, tiled=True)
    query_seg_piece = lax.all_gather(segment_ids, "shard", axis=0, tiled=True)
    count = query_key_piece.shape[0]
    query_block = block_size(count)

    def query_step(index, summed):
        offset = index * query_block
        key_heads = lax.dynamic_slice_in_dim(query_key_piece, offset, query_block, 0).reshape(
            query_block, heads, head_dim
        )
        value_heads = lax.dynamic_slice_in_dim(query_value_piece, offset, query_block, 0).reshape(
            query_block, heads, head_dim
        )
        key_segs = lax.dynamic_slice_in_dim(query_seg_piece, offset, query_block, 0)

        def query_update(summed):
            probs, d_scores = grad_block(
                query_heads,
                dctx_heads,
                log_total,
                delta,
                segment_ids,
                key_heads,
                value_heads,
                key_segs,
            )
            return (
                summed
                + jnp.einsum(
                    "hqk,khd->qhd", d_scores, key_heads, preferred_element_type=jnp.float32
                )
                * scale_factor
            )

        touches = jnp.logical_and(key_segs[0] <= seg_high, key_segs[-1] >= seg_low)
        return lax.cond(touches, query_update, keep_state, summed)

    d_query = lax.fori_loop(0, count // query_block, query_step, zero_heads)
    all_log_total, all_delta = (
        lax.all_gather(log_total, "shard", axis=1, tiled=True),
        lax.all_gather(delta, "shard", axis=1, tiled=True),
    )
    query_piece = lax.all_gather(query, "shard", axis=0, tiled=True)
    dctx_piece = lax.all_gather(d_context, "shard", axis=0, tiled=True)
    key_seg_piece = lax.all_gather(segment_ids, "shard", axis=0, tiled=True)
    count = query_piece.shape[0]
    key_block = block_size(count)

    def key_step(index, state):
        offset = index * key_block
        piece_query = lax.dynamic_slice_in_dim(query_piece, offset, key_block, 0).reshape(
            key_block, heads, head_dim
        )
        piece_dctx = lax.dynamic_slice_in_dim(dctx_piece, offset, key_block, 0).reshape(
            key_block, heads, head_dim
        )
        piece_segs = lax.dynamic_slice_in_dim(key_seg_piece, offset, key_block, 0)
        piece_log = lax.dynamic_slice_in_dim(all_log_total, offset, key_block, 1)
        piece_delta = lax.dynamic_slice_in_dim(all_delta, offset, key_block, 1)

        def key_update(state):
            d_key, d_value = state
            probs, d_scores = grad_block(
                piece_query,
                piece_dctx,
                piece_log,
                piece_delta,
                piece_segs,
                key_local,
                value_local,
                segment_ids,
            )
            d_key = (
                d_key
                + jnp.einsum(
                    "hqk,qhd->khd", d_scores, piece_query, preferred_element_type=jnp.float32
                )
                * scale_factor
            )
            d_value = d_value + jnp.einsum(
                "hqk,qhd->khd", probs, piece_dctx, preferred_element_type=jnp.float32
            )
            return (d_key, d_value)

        touches = jnp.logical_and(piece_segs[0] <= seg_high, piece_segs[-1] >= seg_low)
        return lax.cond(touches, key_update, keep_state, state)

    d_key_heads, d_value_heads = lax.fori_loop(
        0, count // key_block, key_step, (zero_heads, zero_heads)
    )
    d_keys = d_key_heads.reshape(tok_rows, width)
    d_values = d_value_heads.reshape(tok_rows, width)
    d_query = d_query.reshape(tok_rows, width)
    grad_b_qv = jnp.stack([jnp.sum(d_query, axis=0), jnp.sum(d_values, axis=0)], axis=0)
    d_qkv = jnp.concatenate([d_query, d_keys, d_values], axis=1).astype(jnp.bfloat16)
    grad_w_qkv = jnp.einsum("td,te->de", hidden, d_qkv, preferred_element_type=jnp.float32)
    d_hidden = d_resid1 + jnp.einsum(
        "te,de->td", d_qkv, wq_full, preferred_element_type=jnp.float32
    )
    local_grads = (
        grad_w_qkv,
        grad_b_qv,
        grad_w_out,
        grad_b_out,
        grad_gain1,
        grad_shift1,
        grad_w_in,
        grad_b_in,
        grad_w_back,
        grad_b_back,
        grad_gain2,
        grad_shift2,
    )
    shard_grads = (
        lax.psum_scatter(
            local_grads[0].astype(jnp.bfloat16), "shard", scatter_dimension=0, tiled=True
        ).astype(jnp.float32),
        lax.psum_scatter(
            local_grads[1].astype(jnp.bfloat16), "shard", scatter_dimension=1, tiled=True
        ).astype(jnp.float32),
        lax.psum_scatter(
            local_grads[2].astype(jnp.bfloat16), "shard", scatter_dimension=0, tiled=True
        ).astype(jnp.float32),
        lax.psum_scatter(
            local_grads[3].astype(jnp.bfloat16), "shard", scatter_dimension=0, tiled=True
        ).astype(jnp.float32),
        lax.psum_scatter(
            local_grads[4].astype(jnp.bfloat16), "shard", scatter_dimension=0, tiled=True
        ).astype(jnp.float32),
        lax.psum_scatter(
            local_grads[5].astype(jnp.bfloat16), "shard", scatter_dimension=0, tiled=True
        ).astype(jnp.float32),
        lax.psum_scatter(
            local_grads[6].astype(jnp.bfloat16), "shard", scatter_dimension=0, tiled=True
        ).astype(jnp.float32),
        lax.psum_scatter(
            local_grads[7].astype(jnp.bfloat16), "shard", scatter_dimension=0, tiled=True
        ).astype(jnp.float32),
        lax.psum_scatter(
            local_grads[8].astype(jnp.bfloat16), "shard", scatter_dimension=0, tiled=True
        ).astype(jnp.float32),
        lax.psum_scatter(
            local_grads[9].astype(jnp.bfloat16), "shard", scatter_dimension=0, tiled=True
        ).astype(jnp.float32),
        lax.psum_scatter(
            local_grads[10].astype(jnp.bfloat16), "shard", scatter_dimension=0, tiled=True
        ).astype(jnp.float32),
        lax.psum_scatter(
            local_grads[11].astype(jnp.bfloat16), "shard", scatter_dimension=0, tiled=True
        ).astype(jnp.float32),
    )
    total_grads = (
        lax.psum(shard_grads[0].astype(jnp.bfloat16), "replica").astype(jnp.float32),
        lax.psum(shard_grads[1].astype(jnp.bfloat16), "replica").astype(jnp.float32),
        lax.psum(shard_grads[2].astype(jnp.bfloat16), "replica").astype(jnp.float32),
        lax.psum(shard_grads[3].astype(jnp.bfloat16), "replica").astype(jnp.float32),
        lax.psum(shard_grads[4].astype(jnp.bfloat16), "replica").astype(jnp.float32),
        lax.psum(shard_grads[5].astype(jnp.bfloat16), "replica").astype(jnp.float32),
        lax.psum(shard_grads[6].astype(jnp.bfloat16), "replica").astype(jnp.float32),
        lax.psum(shard_grads[7].astype(jnp.bfloat16), "replica").astype(jnp.float32),
        lax.psum(shard_grads[8].astype(jnp.bfloat16), "replica").astype(jnp.float32),
        lax.psum(shard_grads[9].astype(jnp.bfloat16), "replica").astype(jnp.float32),
        lax.psum(shard_grads[10].astype(jnp.bfloat16), "replica").astype(jnp.float32),
        lax.psum(shard_grads[11].astype(jnp.bfloat16), "replica").astype(jnp.float32),
    )
    return (output, d_hidden) + tuple(total_grads)


def solution(mesh):
    in_specs = (
        P(("replica", "shard"), None),
        P(("replica", "shard")),
        P("shard", None),
        P(None, "shard"),
        P("shard", None),
        P("shard"),
        P("shard"),
        P("shard"),
        P("shard", None),
        P("shard"),
        P("shard", None),
        P("shard"),
        P("shard"),
        P("shard"),
        P(("replica", "shard"), None),
    )
    out_specs = (
        P(("replica", "shard"), None),
        P(("replica", "shard"), None),
        P("shard", None),
        P(None, "shard"),
        P("shard", None),
        P("shard"),
        P("shard"),
        P("shard"),
        P("shard", None),
        P("shard"),
        P("shard", None),
        P("shard"),
        P("shard"),
        P("shard"),
    )
    return jax.shard_map(body, mesh=mesh, in_specs=in_specs, out_specs=out_specs, check_vma=False)
```

profile of v0, /device:TPU:0, one launch (start us, length us, event | category | flops | bytes accessed | tf_op | source)
XLA Modules:
  0.0 788.4 jit_solution(2066285224074038387)
XLA Ops:
  8.0 38.5 %all-gather.12.cloned.1.call-done = bf16[768,2304]{1,0:T(8,128)(2,1)} async-done(((bf16[96,2304]{1,0:T(8,128)(2,1)}), bf16[768,2304]{1,0:T(8,128)(2,1)}) %all-gather.12.cloned.1.call-update) | async-done | bytes 3538960 | tf_op jit(solution)/shard_map/all_gather | solution.py:74
  50.7 8.7 %all-gather.1 = bf16[8,96,2]{1,2,0:T(2,128)(2,1)S(1)} all-gather(bf16[1,96,2]{1,2,0:T(2,128)(2,1)S(1)} %bitcast.172), channel_id=1, replica_groups=mesh['shard'=8,'replica'=4] {'shard'}, dimensions={0}, use_global_device_ids=true | all-gather | bytes 3456 | tf_op jit(solution)/shard_map/all_gather | solution.py:76
  64.7 24.2 %all-reduce.14 = (bf16[768]{0:T(1024)(128)(2,1)S(1)}, bf16[768]{0:T(1024)(128)(2,1)S(1)}, bf16[768]{0:T(1024)(128)(2,1)S(1)}, bf16[768]{0:T(1024)(128)(2,1)S(1)}, bf16[768]{0:T(1024)(128)(2,1)S(1)}) all-reduce(bf16[768]{0:T(1024)(128)(2,1)S(1)} %dynamic-update-slice, ...), channel_id=1, replica_groups=mesh['shard'=8,'replica'=4] {'shard'}, use_global_device_ids=true, to_apply=%add | all-reduce | flops 3840 | bytes 15360
  88.8 8.1 %all-gather.2 = bf16[8,1,384]{2,1,0:T(2,128)(2,1)S(1)} all-gather(bf16[1,1,384]{2,1,0:T(2,128)(2,1)S(1)} %reshape.302), channel_id=1, replica_groups=mesh['shard'=8,'replica'=4] {'shard'}, dimensions={0}, use_global_device_ids=true | all-gather | bytes 6912 | tf_op jit(solution)/shard_map/all_gather | solution.py:144
  97.0 8.8 %all-gather = s32[8,1,256]{2,1,0:T(1,128)} all-gather(s32[1,1,256]{2,1,0:T(1,128)S(1)} %bitcast.168), channel_id=1, replica_groups=mesh['shard'=8,'replica'=4] {'shard'}, dimensions={0}, use_global_device_ids=true | all-gather | bytes 9216 | tf_op jit(solution)/shard_map/all_gather | solution.py:96
  122.7 32.9 %while.48 = (s32[]{:T(128)}, f32[12,256]{1,0:T(8,128)S(1)}, f32[12,256]{1,0:T(8,128)S(1)}, f32[256,12,64]{0,2,1:T(8,128)S(1)}, s32[2048]{0:T(1024)}, /*index=5*/...) while((s32[]{:T(128)}, f32[12,256]{1,0:T(8,128)S(1)}, ...), condition=%wide.region_5.6_spmd, body=%wide.region_0.5_spmd.sunk | while | flops 420488192 | bytes 26287476 | solution.py:130
  158.3 25.8 %all-gather.20.cloned.1.call-done = bf16[768,3072]{1,0:T(8,128)(2,1)} async-done(((bf16[96,3072]{1,0:T(8,128)(2,1)}), bf16[768,3072]{1,0:T(8,128)(2,1)}) %all-gather.20.cloned.1.call-update) | async-done | bytes 4718608 | tf_op jit(solution)/shard_map/all_gather | solution.py:143
  184.0 12.1 %multiply_convert_fusion.8 = (bf16[256,3072]{1,0:T(8,128)(2,1)}, f32[256,3072]{1,0:T(8,128)}, f32[256,3072]{1,0:T(8,128)}) fusion(f32[3072]{0:T(1024)S(1)} %bitcast.171, bf16[768,3072]{1,0:T(8,128)(2,1)} %all-gather.20.cloned.1.call-done, f32[256,768]{1,0:T(8,128)S(1)} %get-tuple-element.1246, f32[768]{0:T(1024)S(1)} %convert_element_type.209, ...), kind=kOutput, calls=%fused_computation.63 | convolution fusion | flops 1260847104 | bytes 13389824 | tf_op jit(solution)/shard_map/dot_general | solution.py:151
  196.1 28.4 %all-gather.22.cloned.1.call-done = bf16[3072,768]{1,0:T(8,128)(2,1)} async-done(((bf16[384,768]{1,0:T(8,128)(2,1)}), bf16[3072,768]{1,0:T(8,128)(2,1)}) %all-gather.22.cloned.1.call-update) | async-done | bytes 4718608 | tf_op jit(solution)/shard_map/all_gather | solution.py:145
  242.4 16.2 %all-gather.24.cloned.1.call-done = bf16[2048,768]{1,0:T(8,128)(2,1)} async-done(((bf16[256,768]{1,0:T(8,128)(2,1)}), bf16[2048,768]{1,0:T(8,128)(2,1)}) %all-gather.24.cloned.1.call-update) | async-done | bytes 3145744 | tf_op jit(solution)/shard_map/all_gather | solution.py:230
  264.1 9.3 %all_gather.77 = f32[12,2048]{1,0:T(8,128)S(1)} all-gather(f32[12,256]{1,0:T(8,128)} %log_add_fusion), channel_id=1, replica_groups=mesh['shard'=8,'replica'=4] {'shard'}, dimensions={1}, use_global_device_ids=true | all-gather | bytes 110592 | tf_op jit(solution)/shard_map/all_gather | solution.py:227
  275.1 8.6 %all_gather.79 = f32[12,2048]{1,0:T(8,128)S(1)} all-gather(f32[12,256]{1,0:T(8,128)} %fusion.66), channel_id=1, replica_groups=mesh['shard'=8,'replica'=4] {'shard'}, dimensions={1}, use_global_device_ids=true | all-gather | bytes 110592 | tf_op jit(solution)/shard_map/all_gather | solution.py:228
  284.6 51.7 %while.49 = (s32[]{:T(128)}, f32[256,12,64]{0,2,1:T(8,128)}, s32[2048]{0:T(1024)}, s32[]{:T(128)}, s32[]{:T(128)}, /*index=5*/s32[256]{0:T(256)}, bf16[2048,768]...) while((s32[]{:T(128)}, f32[256,12,64]{0,2,1:T(8,128)}, ...), condition=%wide.region_17.18_spmd, body=%wide.region_14.17_spmd.sunk | while | flops 613941248 | bytes 20745584 | solution.py:225
  288.8 11.8 %conditional.7 = (f32[256,12,64]{0,2,1:T(8,128)}) conditional(s32[]{:T(128)} %convert_element_type.315, f32[256,12,64]{0,2,1:T(8,128)} %get-tuple-element.1570, (s32[256]{0:T(256)}, s32[512]{0:T(512)S(1)}, bf16[2048,768]{0,1:T(8,128)(2,1)}, s32[]{:T(128)}, bf16[256,12,64]{0,2,1:T(8,128)(2,1)S(1)}, /*index=5*/f32[12,256]{1,0:T(8,128)}, ...), branch_computations={%region_15.15_spmd, %region_16.16_spmd} | conditional | flops 613941248 | bytes 20741160 | solution.py:223
  294.2 6.4 fusion.29
  304.7 11.8 %conditional.7 = (f32[256,12,64]{0,2,1:T(8,128)}) conditional(s32[]{:T(128)} %convert_element_type.315, f32[256,12,64]{0,2,1:T(8,128)} %get-tuple-element.1570, (s32[256]{0:T(256)}, s32[512]{0:T(512)S(1)}, bf16[2048,768]{0,1:T(8,128)(2,1)}, s32[]{:T(128)}, bf16[256,12,64]{0,2,1:T(8,128)(2,1)S(1)}, /*index=5*/f32[12,256]{1,0:T(8,128)}, ...), branch_computations={%region_15.15_spmd, %region_16.16_spmd} | conditional | flops 613941248 | bytes 20741160 | solution.py:223
  320.5 11.8 %conditional.7 = (f32[256,12,64]{0,2,1:T(8,128)}) conditional(s32[]{:T(128)} %convert_element_type.315, f32[256,12,64]{0,2,1:T(8,128)} %get-tuple-element.1570, (s32[256]{0:T(256)}, s32[512]{0:T(512)S(1)}, bf16[2048,768]{0,1:T(8,128)(2,1)}, s32[]{:T(128)}, bf16[256,12,64]{0,2,1:T(8,128)(2,1)S(1)}, /*index=5*/f32[12,256]{1,0:T(8,128)}, ...), branch_computations={%region_15.15_spmd, %region_16.16_spmd} | conditional | flops 613941248 | bytes 20741160 | solution.py:223
  325.8 6.4 fusion.29
  342.9 66.5 %while.50 = (s32[]{:T(128)}, f32[256,12,64]{0,2,1:T(8,128)}, f32[256,12,64]{0,2,1:T(8,128)}, s32[2048]{0:T(1024)}, s32[]{:T(128)}, /*index=5*/s32[]{:T(128)}, s3...) while((s32[]{:T(128)}, f32[256,12,64]{0,2,1:T(8,128)}, ...), condition=%wide.region_21.22_spmd, body=%wide.region_18.21_spmd.sunk | while | flops 821755904 | bytes 29670792 | solution.py:275
  346.9 16.9 %conditional.8 = ((f32[256,12,64]{0,2,1:T(8,128)}, f32[256,12,64]{0,2,1:T(8,128)})) conditional(s32[]{:T(128)} %convert_element_type.316, (f32[256,12,64]{0,2,1:T(8,128)}, f32[256,12,64]{0,2,1:T(8,128)}) %tuple.174, (s32[512]{0:T(512)S(1)}, s32[256]{0:T(256)S(1)}, bf16[2048,768]{0,1:T(8,128)(2,1)}, s32[]{:T(128)}, ...), branch_computations={%region_19.19_spmd, %region_20.20_spmd} | conditional | flops 821755904 | bytes 29666336 | solution.py:273
  352.2 6.7 fusion.50
  367.7 16.9 %conditional.8 = ((f32[256,12,64]{0,2,1:T(8,128)}, f32[256,12,64]{0,2,1:T(8,128)})) conditional(s32[]{:T(128)} %convert_element_type.316, (f32[256,12,64]{0,2,1:T(8,128)}, f32[256,12,64]{0,2,1:T(8,128)}) %tuple.174, (s32[512]{0:T(512)S(1)}, s32[256]{0:T(256)S(1)}, bf16[2048,768]{0,1:T(8,128)(2,1)}, s32[]{:T(128)}, ...), branch_computations={%region_19.19_spmd, %region_20.20_spmd} | conditional | flops 821755904 | bytes 29666336 | solution.py:273
  373.1 6.7 fusion.50
  388.6 16.9 %conditional.8 = ((f32[256,12,64]{0,2,1:T(8,128)}, f32[256,12,64]{0,2,1:T(8,128)})) conditional(s32[]{:T(128)} %convert_element_type.316, (f32[256,12,64]{0,2,1:T(8,128)}, f32[256,12,64]{0,2,1:T(8,128)}) %tuple.174, (s32[512]{0:T(512)S(1)}, s32[256]{0:T(256)S(1)}, bf16[2048,768]{0,1:T(8,128)(2,1)}, s32[]{:T(128)}, ...), branch_computations={%region_19.19_spmd, %region_20.20_spmd} | conditional | flops 821755904 | bytes 29666336 | solution.py:273
  393.9 6.7 fusion.50
  440.5 58.1 %reduce-scatter.16.cloned.1.call-done = bf16[96,2304]{1,0:T(8,128)(2,1)} async-done(((bf16[768,2304]{1,0:T(8,128)(2,1)}), bf16[96,2304]{1,0:T(8,128)(2,1)}) %reduce-scatter.16.cloned.1.call-update) | async-done | bytes 442384
  500.8 38.3 %reduce-scatter.10.cloned.1.call-done = bf16[96,768]{1,0:T(8,128)(2,1)} async-done(((bf16[768,768]{1,0:T(8,128)(2,1)}), bf16[96,768]{1,0:T(8,128)(2,1)}) %reduce-scatter.10.cloned.1.call-update) | async-done | bytes 147472 | tf_op jit(solution)/shard_map/reduce_scatter | solution.py:308
  539.1 57.3 %reduce-scatter.12.cloned.1.call-done = bf16[96,3072]{1,0:T(8,128)(2,1)} async-done(((bf16[768,3072]{1,0:T(8,128)(2,1)}), bf16[96,3072]{1,0:T(8,128)(2,1)}) %reduce-scatter.12.cloned.1.call-update) | async-done | bytes 589840 | tf_op jit(solution)/shard_map/reduce_scatter | solution.py:320
  596.3 57.1 %reduce-scatter.14.cloned.1.call-done = bf16[384,768]{1,0:T(8,128)(2,1)} async-done(((bf16[3072,768]{1,0:T(8,128)(2,1)}), bf16[384,768]{1,0:T(8,128)(2,1)}) %reduce-scatter.14.cloned.1.call-update) | async-done | bytes 589840 | tf_op jit(solution)/shard_map/reduce_scatter | solution.py:326
  658.2 23.6 %all-reduce.13 = (bf16[768]{0:T(1024)(128)(2,1)S(1)}, bf16[768]{0:T(1024)(128)(2,1)S(1)}, bf16[768]{0:T(1024)(128)(2,1)S(1)}, bf16[768]{0:T(1024)(128)(2,1)S(1)}...) all-reduce(bf16[768]{0:T(1024)(128)(2,1)} %dynamic-update-slice.5, ...), channel_id=1, replica_groups=mesh['shard'=8,'replica'=4] {'shard'}, use_global_device_ids=true, to_apply=%add.5 | all-reduce | flops 8448 | bytes 33792
  691.5 11.9 %all-reduce.15 = (bf16[2,96]{1,0:T(2,128)(2,1)S(1)}, bf16[96]{0:T(256)(128)(2,1)S(1)}, bf16[96]{0:T(256)(128)(2,1)S(1)}, bf16[96]{0:T(256)(128)(2,1)S(1)}, bf16[...) all-reduce(bf16[2,96]{1,0:T(2,128)(2,1)S(1)} %copy.95, ...), channel_id=1, replica_groups=mesh['shard'=8,'replica'=4] {'replica'}, use_global_device_ids=true, to_apply=%region_27.28 | all-reduce | flops 1152 | bytes 4608 | tf_op jit(solution)/shard_map/psum | solution.py:341
  707.7 66.8 %all-reduce.19.cloned.1.call-done = (bf16[96,2304]{0,1:T(8,128)(2,1)}, bf16[96,768]{1,0:T(8,128)(2,1)}, bf16[96,3072]{1,0:T(8,128)(2,1)}, bf16[384,768]{1,0:T(8,128)(2,1)}) async-done(((bf16[96,2304]{0,1:T(8,128)(2,1)}, bf16[96,768]{1,0:T(8,128)(2,1)}, bf16[96,3072]{1,0:T(8,128)(2,1)}, bf16[384,768]{1,0:T(8,128)(2,1)}), (bf16[96,2304]{0,1:T(8,128)(2,1)}, bf16[96,768]{1,0:T(8,128)(2,1)}, ...) | async-done | bytes 1769488 | tf_op jit(solution)/shard_map/psum | solution.py:340
  (325 shorter events, 221.7 us)
Async XLA Ops:
  7.2 39.3 %all-gather.12.cloned.1.call-start = ((), (), s32[]{:S(2)}) async-start(), calls=%async_computation.5 | async-start | bytes 3981312 | tf_op jit(solution)/shard_map/all_gather | solution.py:74
  7.9 42.7 %copy-start.42 = (bf16[2,96]{1,0:T(2,128)(2,1)S(1)}, bf16[2,96]{1,0:T(2,128)(2,1)}, u32[]{:S(2)}) copy-start(bf16[2,96]{1,0:T(2,128)(2,1)} %param.30) | copy-start | bytes 1156
  7.9 99.1 %all-gather.14.cloned.1.call-start = ((), (), s32[]{:S(2)}) async-start(), calls=%async_computation.6 | async-start | bytes 3538944 | tf_op jit(solution)/shard_map/all_gather | solution.py:94
  49.8 14.7 %copy-start.47 = (bf16[96]{0:T(256)(128)(2,1)S(1)}, bf16[96]{0:T(256)(128)(2,1)}, u32[]{:S(2)}) copy-start(bf16[96]{0:T(256)(128)(2,1)} %param.39) | copy-start | bytes 580
  49.8 39.1 %copy-start.41 = (bf16[384]{0:T(512)(128)(2,1)S(1)}, bf16[384]{0:T(512)(128)(2,1)}, u32[]{:S(2)}) copy-start(bf16[384]{0:T(512)(128)(2,1)} %param.36) | copy-start | bytes 2308
  49.8 47.2 %copy-start.20 = (s32[256]{0:T(256)S(1)}, s32[256]{0:T(256)}, u32[]{:S(2)}) copy-start(s32[256]{0:T(256)} %param.28) | copy-start | bytes 3076
  50.6 67.2 %all-gather.16.cloned.1.call-start = ((), (), s32[]{:S(2)}) async-start(), calls=%async_computation.7 | async-start | bytes 3538944 | tf_op jit(solution)/shard_map/all_gather | solution.py:95
  60.4 46.3 %copy-start.7 = (bf16[256,768]{1,0:T(8,128)(2,1)}, bf16[256,768]{1,0:T(8,128)(2,1)S(1)}, u32[]{:S(2)}) copy-start(bf16[256,768]{1,0:T(8,128)(2,1)S(1)} %get-tuple-element.1236) | copy-start | bytes 1179652
  60.4 95.2 %all-gather.18.cloned.1.call-start = ((), (), s32[]{:S(2)}) async-start(), calls=%async_computation.8 | async-start | bytes 1327104 | tf_op jit(solution)/shard_map/all_gather | solution.py:75
  61.0 123.0 %all-gather.20.cloned.1.call-start = ((), (), s32[]{:S(2)}) async-start(), calls=%async_computation.9 | async-start | bytes 5308416 | tf_op jit(solution)/shard_map/all_gather | solution.py:143
  61.6 163.0 %all-gather.22.cloned.1.call-start = ((), (), s32[]{:S(2)}) async-start(), calls=%async_computation.10 | async-start | bytes 5308416 | tf_op jit(solution)/shard_map/all_gather | solution.py:145
  62.2 196.5 %all-gather.24.cloned.1.call-start = ((), (), s32[]{:S(2)}) async-start(), calls=%async_computation.11 | async-start | bytes 3538944 | tf_op jit(solution)/shard_map/all_gather | solution.py:230
  97.0 127.6 %copy-start.25 = (f32[768]{0:T(1024)}, f32[768]{0:T(1024)S(1)}, u32[]{:S(2)}) copy-start(f32[768]{0:T(1024)S(1)} %convert_element_type.209) | copy-start | bytes 9220
  97.0 139.6 %copy-start.23 = (f32[768]{0:T(1024)}, f32[768]{0:T(1024)S(1)}, u32[]{:S(2)}) copy-start(f32[768]{0:T(1024)S(1)} %convert_element_type.208) | copy-start | bytes 9220
  97.0 133.3 %copy-start.27 = (f32[768]{0:T(1024)}, f32[768]{0:T(1024)S(1)}, u32[]{:S(2)}) copy-start(f32[768]{0:T(1024)S(1)} %convert_element_type.214) | copy-start | bytes 9220
  106.7 229.7 %all-gather.26.cloned.1.call-start = ((), (), s32[]{:S(2)}) async-start(), calls=%async_computation.12 | async-start | bytes 3538944 | tf_op jit(solution)/shard_map/all_gather | solution.py:231
  122.6 33.5 %copy-start.12 = (bf16[256,768]{1,0:T(8,128)(2,1)S(1)}, bf16[256,768]{1,0:T(8,128)(2,1)}, u32[]{:S(2)}) copy-start(bf16[256,768]{1,0:T(8,128)(2,1)} %param.27) | copy-start | bytes 1179652
  155.6 40.5 %copy-start.9 = (bf16[256,12,64]{0,2,1:T(8,128)(2,1)}, bf16[256,12,64]{0,2,1:T(8,128)(2,1)S(1)}, u32[]{:S(2)}) copy-start(bf16[256,12,64]{0,2,1:T(8,128)(2,1)S(1)} %fusion.70) | copy-start | bytes 1179652
  158.0 78.6 %copy-start.31 = (f32[256]{0:T(256)}, f32[256]{0:T(256)S(1)}, u32[]{:S(2)}) copy-start(f32[256]{0:T(256)S(1)} %broadcast_multiply_fusion.1) | copy-start | bytes 3076
  158.3 78.4 %copy-start.36 = (f32[256]{0:T(256)}, f32[256]{0:T(256)S(1)}, u32[]{:S(2)}) copy-start(f32[256]{0:T(256)S(1)} %fusion.71) | copy-start | bytes 3076
  237.0 26.5 %copy-start.2 = (f32[256,768]{1,0:T(8,128)}, f32[256,768]{1,0:T(8,128)S(1)}, u32[]{:S(2)}) copy-start(f32[256,768]{1,0:T(8,128)S(1)} %get-tuple-element.1214) | copy-start | bytes 2359300
  238.3 260.4 %reduce-scatter.16.cloned.1.call-start = ((), (), s32[]{:S(2)}) async-start(), calls=%async_computation.16 | async-start | bytes 3981312
  242.4 21.0 %copy-start.16 = (f32[12,256]{1,0:T(8,128)S(1)}, f32[12,256]{1,0:T(8,128)}, u32[]{:S(2)}) copy-start(f32[12,256]{1,0:T(8,128)} %copy-done.15) | copy-start | bytes 36868
  422.3 116.8 %reduce-scatter.10.cloned.1.call-start = ((), (), s32[]{:S(2)}) async-start(), calls=%async_computation.13 | async-start | bytes 1327104 | tf_op jit(solution)/shard_map/reduce_scatter | solution.py:308
  425.1 171.3 %reduce-scatter.12.cloned.1.call-start = ((), (), s32[]{:S(2)}) async-start(), calls=%async_computation.14 | async-start | bytes 5308416 | tf_op jit(solution)/shard_map/reduce_scatter | solution.py:320
  430.5 222.9 %reduce-scatter.14.cloned.1.call-start = ((), (), s32[]{:S(2)}) async-start(), calls=%async_computation.15 | async-start | bytes 5308416 | tf_op jit(solution)/shard_map/reduce_scatter | solution.py:326
  436.7 245.6 %copy-start.1 = (f32[256,768]{1,0:T(8,128)S(1)}, f32[256,768]{1,0:T(8,128)}, u32[]{:S(2)}) copy-start(f32[256,768]{1,0:T(8,128)} %copy-done) | copy-start | bytes 2359300
  436.7 245.6 %copy-start.28 = (f32[768]{0:T(1024)S(1)}, f32[768]{0:T(1024)}, u32[]{:S(2)}) copy-start(f32[768]{0:T(1024)} %copy-done.27) | copy-start | bytes 9220
  436.8 245.6 %copy-start.30 = (f32[256]{0:T(256)S(1)}, f32[256]{0:T(256)}, u32[]{:S(2)}) copy-start(f32[256]{0:T(256)} %copy-done.29) | copy-start | bytes 3076
  436.8 247.1 %copy-start.19 = (bf16[256,12,64]{0,2,1:T(8,128)(2,1)S(1)}, bf16[256,12,64]{0,2,1:T(8,128)(2,1)}, u32[]{:S(2)}) copy-start(bf16[256,12,64]{0,2,1:T(8,128)(2,1)} %copy-done.18) | copy-start | bytes 1179652
  436.8 254.0 %reduce-scatter.18.cloned.1.call-start = ((), (), s32[]{:S(2)}) async-start(), calls=%async_computation.17 | async-start | bytes 221184
  440.5 334.0 %all-reduce.19.cloned.1.call-start = ((), (), s32[]{:S(2)}) async-start(), calls=%async_computation.18 | async-start | bytes 3833856 | tf_op jit(solution)/shard_map/psum | solution.py:340
  (38 other events, 183.0 us)
Sparse Core Ops, SparseCore 0:
  9.9 36.5 all-gather.11
  50.7 32.3 all-gather.13
  85.6 32.1 all-gather.15
  119.5 23.9 all-gather.17
  145.2 38.7 all-gather.19
  185.8 38.7 all-gather.21
  226.5 32.1 all-gather.23
  260.6 32.3 all-gather.25
  422.4 76.2 reduce-scatter.15
  502.3 36.6 reduce-scatter.9
  542.5 53.7 reduce-scatter.11
  599.6 53.7 reduce-scatter.13
  657.1 33.6 reduce-scatter.17
  693.8 80.6 all-reduce.18
where the time goes:
time: 794 us; the launch traced here: 788 us
  waiting for transfers between devices  398 us (50%)
  matrix products  130 us (16%)
  blocking collectives  103 us (13%)
  local copies, waits for them, and re-layouts  79.1 us (10%)
  loops' own time  32.1 us (4%)
  other arithmetic  27.6 us (3%)
  between operations  16.9 us (2%)
    psum x1, waiting for transfers between devices, body(): lax.psum(shard_grads[0].astype(jnp.bfloat16), 'replica').astype(jnp.float32)  66.8 us
    unnamed x16, waiting for transfers between devices  63.4 us
    reduce_scatter x1, waiting for transfers between devices, body(): lax.psum_scatter(local_grads[6].astype(jnp.bfloat16), 'shard', scatter_di...  57.3 us
    reduce_scatter x1, waiting for transfers between devices, body(): lax.psum_scatter(local_grads[8].astype(jnp.bfloat16), 'shard', scatter_di...  57.1 us
    unnamed x2, blocking collectives  47.7 us
    all_gather x1, waiting for transfers between devices, body(): lax.all_gather(w_qkv, 'shard', axis=0, tiled=True)  38.5 us
    reduce_scatter x1, waiting for transfers between devices, body(): lax.psum_scatter(local_grads[2].astype(jnp.bfloat16), 'shard', scatter_di...  38.3 us
    all_gather x1, waiting for transfers between devices, body(): lax.all_gather(w_back, 'shard', axis=0, tiled=True)  28.4 us
  transfers between devices with their start and end apart: 14, of which 11 were waited for; matrix products, arithmetic and copies ran while one was open for 19% of the time, Pallas kernels for 0%

commit v1 on v0

--- a/solution.py
+++ b/solution.py
@@ -227,8 +227,11 @@
         lax.all_gather(log_total, "shard", axis=1, tiled=True),
         lax.all_gather(delta, "shard", axis=1, tiled=True),
     )
-    query_piece = lax.all_gather(query, "shard", axis=0, tiled=True)
-    dctx_piece = lax.all_gather(d_context, "shard", axis=0, tiled=True)
+    query_piece, dctx_piece = jnp.split(
+        lax.all_gather(jnp.concatenate([query, d_context], axis=1), "shard", axis=0, tiled=True),
+        [query.shape[1]],
+        axis=1,
+    )
     key_seg_piece = lax.all_gather(segment_ids, "shard", axis=0, tiled=True)
     count = query_piece.shape[0]
     key_block = block_size(count)

time: 794 us -> 786 us (0.990)
  waiting for transfers between devices: 398 us -> 385 us
    all_gather x2 -> x1, waiting for transfers between devices: 16.3 us -> 0.02 us  [body(): lax.all_gather(jnp.concatenate([query, d_context], axis=1), 'shard', axis...]
    unnamed x16 -> x15, waiting for transfers between devices: 63.4 us -> 63.3 us
  transfers between devices with their start and end apart: 14 -> 13, of which waited for: 11 -> 10; matrix products, arithmetic and copies ran while one was open for 19% -> 16% of each run, Pallas kernels for 0% -> 0%
where the time goes in v1:
time: 786 us; the launch traced here: 781 us
  waiting for transfers between devices  385 us (49%)
  matrix products  130 us (17%)
  blocking collectives  104 us (13%)
  local copies, waits for them, and re-layouts  82.7 us (11%)
  loops' own time  31.8 us (4%)
  other arithmetic  29.4 us (4%)
  between operations  16.9 us (2%)
    psum x1, waiting for transfers between devices, body(): lax.psum(shard_grads[0].astype(jnp.bfloat16), 'replica').astype(jnp.float32)  66.9 us
    unnamed x15, waiting for transfers between devices  63.3 us
    reduce_scatter x1, waiting for transfers between devices, body(): lax.psum_scatter(local_grads[8].astype(jnp.bfloat16), 'shard', scatter_di...  57.3 us
    reduce_scatter x1, waiting for transfers between devices, body(): lax.psum_scatter(local_grads[6].astype(jnp.bfloat16), 'shard', scatter_di...  57.1 us
    unnamed x2, blocking collectives  47.8 us
    all_gather x1, waiting for transfers between devices, body(): lax.all_gather(w_qkv, 'shard', axis=0, tiled=True)  38.5 us
    reduce_scatter x1, waiting for transfers between devices, body(): lax.psum_scatter(local_grads[2].astype(jnp.bfloat16), 'shard', scatter_di...  38.5 us
    all_gather x1, waiting for transfers between devices, body(): lax.all_gather(w_in, 'shard', axis=0, tiled=True)  28.8 us
  transfers between devices with their start and end apart: 13, of which 10 were waited for; matrix products, arithmetic and copies ran while one was open for 16% of the time, Pallas kernels for 0%

profile of v1, /device:TPU:0, one launch (start us, length us, event | category | flops | bytes accessed | tf_op | source)
XLA Modules:
  0.0 780.5 jit_solution(13380063827824222608)
XLA Ops:
  8.0 38.5 %all-gather.11.cloned.1.call-done = bf16[768,2304]{1,0:T(8,128)(2,1)} async-done(((bf16[96,2304]{1,0:T(8,128)(2,1)}), bf16[768,2304]{1,0:T(8,128)(2,1)}) %all-gather.11.cloned.1.call-update) | async-done | bytes 3538960 | tf_op jit(solution)/shard_map/all_gather | solution.py:74
  50.7 8.7 %all-gather.1 = bf16[8,96,2]{1,2,0:T(2,128)(2,1)S(1)} all-gather(bf16[1,96,2]{1,2,0:T(2,128)(2,1)S(1)} %bitcast.173), channel_id=1, replica_groups=mesh['shard'=8,'replica'=4] {'shard'}, dimensions={0}, use_global_device_ids=true | all-gather | bytes 3456 | tf_op jit(solution)/shard_map/all_gather | solution.py:76
  64.7 24.2 %all-reduce.14 = (bf16[768]{0:T(1024)(128)(2,1)S(1)}, bf16[768]{0:T(1024)(128)(2,1)S(1)}, bf16[768]{0:T(1024)(128)(2,1)S(1)}, bf16[768]{0:T(1024)(128)(2,1)S(1)}, bf16[768]{0:T(1024)(128)(2,1)S(1)}) all-reduce(bf16[768]{0:T(1024)(128)(2,1)S(1)} %dynamic-update-slice, ...), channel_id=1, replica_groups=mesh['shard'=8,'replica'=4] {'shard'}, use_global_device_ids=true, to_apply=%add | all-reduce | flops 3840 | bytes 15360
  88.8 8.1 %all-gather.2 = bf16[8,1,384]{2,1,0:T(2,128)(2,1)S(1)} all-gather(bf16[1,1,384]{2,1,0:T(2,128)(2,1)S(1)} %reshape.302), channel_id=1, replica_groups=mesh['shard'=8,'replica'=4] {'shard'}, dimensions={0}, use_global_device_ids=true | all-gather | bytes 6912 | tf_op jit(solution)/shard_map/all_gather | solution.py:144
  97.0 9.1 %all-gather = s32[8,1,256]{2,1,0:T(1,128)S(1)} all-gather(s32[1,1,256]{2,1,0:T(1,128)S(1)} %bitcast.168), channel_id=1, replica_groups=mesh['shard'=8,'replica'=4] {'shard'}, dimensions={0}, use_global_device_ids=true | all-gather | bytes 9216 | tf_op jit(solution)/shard_map/all_gather | solution.py:96
  122.6 30.1 %while.48 = (s32[]{:T(128)}, f32[12,256]{1,0:T(8,128)S(1)}, f32[12,256]{1,0:T(8,128)S(1)}, f32[256,12,64]{0,2,1:T(8,128)S(1)}, s32[2048]{0:T(1024)S(1)}, /*index...) while((s32[]{:T(128)}, f32[12,256]{1,0:T(8,128)S(1)}, ...), condition=%wide.region_5.6_spmd, body=%wide.region_0.5_spmd.sunk | while | flops 420488192 | bytes 26287476 | solution.py:130
  155.2 28.8 %all-gather.19.cloned.1.call-done = bf16[768,3072]{1,0:T(8,128)(2,1)} async-done(((bf16[96,3072]{1,0:T(8,128)(2,1)}), bf16[768,3072]{1,0:T(8,128)(2,1)}) %all-gather.19.cloned.1.call-update) | async-done | bytes 4718608 | tf_op jit(solution)/shard_map/all_gather | solution.py:143
  184.0 12.1 %multiply_convert_fusion.8 = (bf16[256,3072]{1,0:T(8,128)(2,1)}, f32[256,3072]{1,0:T(8,128)}, f32[256,3072]{1,0:T(8,128)}) fusion(f32[3072]{0:T(1024)S(1)} %bitcast.172, bf16[768,3072]{1,0:T(8,128)(2,1)} %all-gather.19.cloned.1.call-done, f32[256,768]{1,0:T(8,128)S(1)} %get-tuple-element.1248, f32[768]{0:T(1024)S(1)} %convert_element_type.209, ...), kind=kOutput, calls=%fused_computation.63 | convolution fusion | flops 1260847104 | bytes 13389824 | tf_op jit(solution)/shard_map/dot_general | solution.py:151
  196.2 28.4 %all-gather.21.cloned.1.call-done = bf16[3072,768]{1,0:T(8,128)(2,1)} async-done(((bf16[384,768]{1,0:T(8,128)(2,1)}), bf16[3072,768]{1,0:T(8,128)(2,1)}) %all-gather.21.cloned.1.call-update) | async-done | bytes 4718608 | tf_op jit(solution)/shard_map/all_gather | solution.py:145
  245.0 9.6 %all_gather.74 = f32[12,2048]{1,0:T(8,128)S(1)} all-gather(f32[12,256]{1,0:T(8,128)} %log_add_fusion), channel_id=1, replica_groups=mesh['shard'=8,'replica'=4] {'shard'}, dimensions={1}, use_global_device_ids=true | all-gather | bytes 110592 | tf_op jit(solution)/shard_map/all_gather | solution.py:227
  256.3 8.4 %all_gather.75 = f32[12,2048]{1,0:T(8,128)S(1)} all-gather(f32[12,256]{1,0:T(8,128)} %fusion.66), channel_id=1, replica_groups=mesh['shard'=8,'replica'=4] {'shard'}, dimensions={1}, use_global_device_ids=true | all-gather | bytes 110592 | tf_op jit(solution)/shard_map/all_gather | solution.py:228
  265.7 51.1 %while.49 = (s32[]{:T(128)}, f32[256,12,64]{0,2,1:T(8,128)}, s32[2048]{0:T(1024)}, s32[]{:T(128)}, s32[]{:T(128)}, /*index=5*/s32[256]{0:T(256)}, bf16[2048,768]...) while((s32[]{:T(128)}, f32[256,12,64]{0,2,1:T(8,128)}, ...), condition=%wide.region_17.18_spmd, body=%wide.region_14.17_spmd.sunk | while | flops 613941248 | bytes 20745584 | solution.py:225
  269.8 11.8 %conditional.7 = (f32[256,12,64]{0,2,1:T(8,128)}) conditional(s32[]{:T(128)} %convert_element_type.315, f32[256,12,64]{0,2,1:T(8,128)} %get-tuple-element.1572, (s32[256]{0:T(256)}, s32[512]{0:T(512)S(1)}, bf16[2048,768]{0,1:T(8,128)(2,1)}, s32[]{:T(128)}, bf16[256,12,64]{0,2,1:T(8,128)(2,1)S(1)}, /*index=5*/f32[12,256]{1,0:T(8,128)}, ...), branch_computations={%region_15.15_spmd, %region_16.16_spmd} | conditional | flops 613941248 | bytes 20741160 | solution.py:223
  275.1 6.5 fusion.29
  285.5 11.8 %conditional.7 = (f32[256,12,64]{0,2,1:T(8,128)}) conditional(s32[]{:T(128)} %convert_element_type.315, f32[256,12,64]{0,2,1:T(8,128)} %get-tuple-element.1572, (s32[256]{0:T(256)}, s32[512]{0:T(512)S(1)}, bf16[2048,768]{0,1:T(8,128)(2,1)}, s32[]{:T(128)}, bf16[256,12,64]{0,2,1:T(8,128)(2,1)S(1)}, /*index=5*/f32[12,256]{1,0:T(8,128)}, ...), branch_computations={%region_15.15_spmd, %region_16.16_spmd} | conditional | flops 613941248 | bytes 20741160 | solution.py:223
  290.8 6.4 fusion.29
  301.1 11.8 %conditional.7 = (f32[256,12,64]{0,2,1:T(8,128)}) conditional(s32[]{:T(128)} %convert_element_type.315, f32[256,12,64]{0,2,1:T(8,128)} %get-tuple-element.1572, (s32[256]{0:T(256)}, s32[512]{0:T(512)S(1)}, bf16[2048,768]{0,1:T(8,128)(2,1)}, s32[]{:T(128)}, bf16[256,12,64]{0,2,1:T(8,128)(2,1)S(1)}, /*index=5*/f32[12,256]{1,0:T(8,128)}, ...), branch_computations={%region_15.15_spmd, %region_16.16_spmd} | conditional | flops 613941248 | bytes 20741160 | solution.py:223
  306.5 6.4 fusion.29
  334.3 66.9 %while.50 = (s32[]{:T(128)}, f32[256,12,64]{0,2,1:T(8,128)}, f32[256,12,64]{0,2,1:T(8,128)}, s32[2048]{0:T(1024)}, s32[]{:T(128)}, /*index=5*/s32[]{:T(128)}, s3...) while((s32[]{:T(128)}, f32[256,12,64]{0,2,1:T(8,128)}, ...), condition=%wide.region_21.22_spmd, body=%wide.region_18.21_spmd.sunk | while | flops 821755904 | bytes 29670792 | solution.py:278
  338.2 17.0 %conditional.8 = ((f32[256,12,64]{0,2,1:T(8,128)}, f32[256,12,64]{0,2,1:T(8,128)})) conditional(s32[]{:T(128)} %convert_element_type.316, (f32[256,12,64]{0,2,1:T(8,128)}, f32[256,12,64]{0,2,1:T(8,128)}) %tuple.175, (s32[512]{0:T(512)S(1)}, s32[256]{0:T(256)S(1)}, bf16[2048,768]{0,1:T(8,128)(2,1)}, s32[]{:T(128)}, ...), branch_computations={%region_19.19_spmd, %region_20.20_spmd} | conditional | flops 821755904 | bytes 29666336 | solution.py:276
  343.6 6.8 fusion.50
  359.2 17.0 %conditional.8 = ((f32[256,12,64]{0,2,1:T(8,128)}, f32[256,12,64]{0,2,1:T(8,128)})) conditional(s32[]{:T(128)} %convert_element_type.316, (f32[256,12,64]{0,2,1:T(8,128)}, f32[256,12,64]{0,2,1:T(8,128)}) %tuple.175, (s32[512]{0:T(512)S(1)}, s32[256]{0:T(256)S(1)}, bf16[2048,768]{0,1:T(8,128)(2,1)}, s32[]{:T(128)}, ...), branch_computations={%region_19.19_spmd, %region_20.20_spmd} | conditional | flops 821755904 | bytes 29666336 | solution.py:276
  364.5 6.8 fusion.50
  380.2 17.0 %conditional.8 = ((f32[256,12,64]{0,2,1:T(8,128)}, f32[256,12,64]{0,2,1:T(8,128)})) conditional(s32[]{:T(128)} %convert_element_type.316, (f32[256,12,64]{0,2,1:T(8,128)}, f32[256,12,64]{0,2,1:T(8,128)}) %tuple.175, (s32[512]{0:T(512)S(1)}, s32[256]{0:T(256)S(1)}, bf16[2048,768]{0,1:T(8,128)(2,1)}, s32[]{:T(128)}, ...), branch_computations={%region_19.19_spmd, %region_20.20_spmd} | conditional | flops 821755904 | bytes 29666336 | solution.py:276
  385.5 6.8 fusion.50
  432.3 58.4 %reduce-scatter.16.cloned.1.call-done = bf16[96,2304]{1,0:T(8,128)(2,1)} async-done(((bf16[768,2304]{1,0:T(8,128)(2,1)}), bf16[96,2304]{1,0:T(8,128)(2,1)}) %reduce-scatter.16.cloned.1.call-update) | async-done | bytes 442384
  492.7 38.5 %reduce-scatter.10.cloned.1.call-done = bf16[96,768]{1,0:T(8,128)(2,1)} async-done(((bf16[768,768]{1,0:T(8,128)(2,1)}), bf16[96,768]{1,0:T(8,128)(2,1)}) %reduce-scatter.10.cloned.1.call-update) | async-done | bytes 147472 | tf_op jit(solution)/shard_map/reduce_scatter | solution.py:311
  531.2 57.1 %reduce-scatter.12.cloned.1.call-done = bf16[96,3072]{1,0:T(8,128)(2,1)} async-done(((bf16[768,3072]{1,0:T(8,128)(2,1)}), bf16[96,3072]{1,0:T(8,128)(2,1)}) %reduce-scatter.12.cloned.1.call-update) | async-done | bytes 589840 | tf_op jit(solution)/shard_map/reduce_scatter | solution.py:323
  588.3 57.3 %reduce-scatter.14.cloned.1.call-done = bf16[384,768]{1,0:T(8,128)(2,1)} async-done(((bf16[3072,768]{1,0:T(8,128)(2,1)}), bf16[384,768]{1,0:T(8,128)(2,1)}) %reduce-scatter.14.cloned.1.call-update) | async-done | bytes 589840 | tf_op jit(solution)/shard_map/reduce_scatter | solution.py:329
  650.3 23.6 %all-reduce.13 = (bf16[768]{0:T(1024)(128)(2,1)S(1)}, bf16[768]{0:T(1024)(128)(2,1)S(1)}, bf16[768]{0:T(1024)(128)(2,1)S(1)}, bf16[768]{0:T(1024)(128)(2,1)S(1)}...) all-reduce(bf16[768]{0:T(1024)(128)(2,1)} %dynamic-update-slice.5, ...), channel_id=1, replica_groups=mesh['shard'=8,'replica'=4] {'shard'}, use_global_device_ids=true, to_apply=%add.5 | all-reduce | flops 8448 | bytes 33792
  683.5 12.0 %all-reduce.15 = (bf16[2,96]{1,0:T(2,128)(2,1)S(1)}, bf16[96]{0:T(256)(128)(2,1)S(1)}, bf16[96]{0:T(256)(128)(2,1)S(1)}, bf16[96]{0:T(256)(128)(2,1)S(1)}, bf16[...) all-reduce(bf16[2,96]{1,0:T(2,128)(2,1)S(1)} %copy.95, ...), channel_id=1, replica_groups=mesh['shard'=8,'replica'=4] {'replica'}, use_global_device_ids=true, to_apply=%region_27.28 | all-reduce | flops 1152 | bytes 4608 | tf_op jit(solution)/shard_map/psum | solution.py:344
  699.7 66.9 %all-reduce.19.cloned.1.call-done = (bf16[96,2304]{0,1:T(8,128)(2,1)}, bf16[96,768]{1,0:T(8,128)(2,1)}, bf16[96,3072]{1,0:T(8,128)(2,1)}, bf16[384,768]{1,0:T(8,128)(2,1)}) async-done(((bf16[96,2304]{0,1:T(8,128)(2,1)}, bf16[96,768]{1,0:T(8,128)(2,1)}, bf16[96,3072]{1,0:T(8,128)(2,1)}, bf16[384,768]{1,0:T(8,128)(2,1)}), (bf16[96,2304]{0,1:T(8,128)(2,1)}, bf16[96,768]{1,0:T(8,128)(2,1)}, ...) | async-done | bytes 1769488 | tf_op jit(solution)/shard_map/psum | solution.py:343
  (324 shorter events, 219.6 us)
Async XLA Ops:
  7.2 39.3 %all-gather.11.cloned.1.call-start = ((), (), s32[]{:S(2)}) async-start(), calls=%async_computation.5 | async-start | bytes 3981312 | tf_op jit(solution)/shard_map/all_gather | solution.py:74
  7.9 42.7 %copy-start.42 = (bf16[2,96]{1,0:T(2,128)(2,1)S(1)}, bf16[2,96]{1,0:T(2,128)(2,1)}, u32[]{:S(2)}) copy-start(bf16[2,96]{1,0:T(2,128)(2,1)} %param.30) | copy-start | bytes 1156
  7.9 99.0 %all-gather.13.cloned.1.call-start = ((), (), s32[]{:S(2)}) async-start(), calls=%async_computation.6 | async-start | bytes 3538944 | tf_op jit(solution)/shard_map/all_gather | solution.py:94
  49.7 14.2 %copy-start.45 = (bf16[96]{0:T(256)(128)(2,1)S(1)}, bf16[96]{0:T(256)(128)(2,1)}, u32[]{:S(2)}) copy-start(bf16[96]{0:T(256)(128)(2,1)} %param.33) | copy-start | bytes 580
  49.7 14.4 %copy-start.46 = (bf16[96]{0:T(256)(128)(2,1)S(1)}, bf16[96]{0:T(256)(128)(2,1)}, u32[]{:S(2)}) copy-start(bf16[96]{0:T(256)(128)(2,1)} %param.38) | copy-start | bytes 580
  49.8 14.7 %copy-start.47 = (bf16[96]{0:T(256)(128)(2,1)S(1)}, bf16[96]{0:T(256)(128)(2,1)}, u32[]{:S(2)}) copy-start(bf16[96]{0:T(256)(128)(2,1)} %param.39) | copy-start | bytes 580
  49.8 39.1 %copy-start.41 = (bf16[384]{0:T(512)(128)(2,1)S(1)}, bf16[384]{0:T(512)(128)(2,1)}, u32[]{:S(2)}) copy-start(bf16[384]{0:T(512)(128)(2,1)} %param.36) | copy-start | bytes 2308
  49.8 47.2 %copy-start.19 = (s32[256]{0:T(256)S(1)}, s32[256]{0:T(256)}, u32[]{:S(2)}) copy-start(s32[256]{0:T(256)} %param.28) | copy-start | bytes 3076
  50.6 67.2 %all-gather.15.cloned.1.call-start = ((), (), s32[]{:S(2)}) async-start(), calls=%async_computation.7 | async-start | bytes 3538944 | tf_op jit(solution)/shard_map/all_gather | solution.py:95
  60.4 92.4 %all-gather.17.cloned.1.call-start = ((), (), s32[]{:S(2)}) async-start(), calls=%async_computation.8 | async-start | bytes 1327104 | tf_op jit(solution)/shard_map/all_gather | solution.py:75
  61.0 123.0 %all-gather.19.cloned.1.call-start = ((), (), s32[]{:S(2)}) async-start(), calls=%async_computation.9 | async-start | bytes 5308416 | tf_op jit(solution)/shard_map/all_gather | solution.py:143
  61.6 163.0 %all-gather.21.cloned.1.call-start = ((), (), s32[]{:S(2)}) async-start(), calls=%async_computation.10 | async-start | bytes 5308416 | tf_op jit(solution)/shard_map/all_gather | solution.py:145
  62.1 254.7 %all-gather.23.cloned.1.call-start = ((), (), s32[]{:S(2)}) async-start(), calls=%async_computation.11 | async-start | bytes 7077888 | tf_op jit(solution)/shard_map/all_gather | solution.py:231
  97.0 127.6 %copy-start.25 = (f32[768]{0:T(1024)}, f32[768]{0:T(1024)S(1)}, u32[]{:S(2)}) copy-start(f32[768]{0:T(1024)S(1)} %convert_element_type.209) | copy-start | bytes 9220
  97.0 139.6 %copy-start.23 = (f32[768]{0:T(1024)}, f32[768]{0:T(1024)S(1)}, u32[]{:S(2)}) copy-start(f32[768]{0:T(1024)S(1)} %convert_element_type.208) | copy-start | bytes 9220
  97.0 133.3 %copy-start.27 = (f32[768]{0:T(1024)}, f32[768]{0:T(1024)S(1)}, u32[]{:S(2)}) copy-start(f32[768]{0:T(1024)S(1)} %convert_element_type.214) | copy-start | bytes 9220
  122.6 30.3 %copy-start.12 = (bf16[256,768]{1,0:T(8,128)(2,1)S(1)}, bf16[256,768]{1,0:T(8,128)(2,1)}, u32[]{:S(2)}) copy-start(bf16[256,768]{1,0:T(8,128)(2,1)} %param.27) | copy-start | bytes 1179652
  152.7 43.4 %copy-start.15 = (f32[12,256]{1,0:T(8,128)}, f32[12,256]{1,0:T(8,128)S(1)}, u32[]{:S(2)}) copy-start(f32[12,256]{1,0:T(8,128)S(1)} %get-tuple-element.901) | copy-start | bytes 36868
  152.7 43.4 %copy-start.22 = (s32[2048]{0:T(1024)}, s32[2048]{0:T(1024)S(1)}, u32[]{:S(2)}) copy-start(s32[2048]{0:T(1024)S(1)} %get-tuple-element.1721) | copy-start | bytes 24580
  152.8 43.3 %copy-start.8 = (bf16[256,12,64]{0,2,1:T(8,128)(2,1)}, bf16[256,12,64]{0,2,1:T(8,128)(2,1)S(1)}, u32[]{:S(2)}) copy-start(bf16[256,12,64]{0,2,1:T(8,128)(2,1)S(1)} %fusion.70) | copy-start | bytes 1179652
  155.0 81.6 %copy-start.31 = (f32[256]{0:T(256)}, f32[256]{0:T(256)S(1)}, u32[]{:S(2)}) copy-start(f32[256]{0:T(256)S(1)} %broadcast_multiply_fusion.1) | copy-start | bytes 3076
  155.2 81.4 %copy-start.36 = (f32[256]{0:T(256)}, f32[256]{0:T(256)S(1)}, u32[]{:S(2)}) copy-start(f32[256]{0:T(256)S(1)} %fusion.71) | copy-start | bytes 3076
  239.6 251.0 %reduce-scatter.16.cloned.1.call-start = ((), (), s32[]{:S(2)}) async-start(), calls=%async_computation.15 | async-start | bytes 3981312
  414.1 117.1 %reduce-scatter.10.cloned.1.call-start = ((), (), s32[]{:S(2)}) async-start(), calls=%async_computation.12 | async-start | bytes 1327104 | tf_op jit(solution)/shard_map/reduce_scatter | solution.py:311
  416.8 171.5 %reduce-scatter.12.cloned.1.call-start = ((), (), s32[]{:S(2)}) async-start(), calls=%async_computation.13 | async-start | bytes 5308416 | tf_op jit(solution)/shard_map/reduce_scatter | solution.py:323
  422.3 223.3 %reduce-scatter.14.cloned.1.call-start = ((), (), s32[]{:S(2)}) async-start(), calls=%async_computation.14 | async-start | bytes 5308416 | tf_op jit(solution)/shard_map/reduce_scatter | solution.py:329
  428.5 246.0 %copy-start.1 = (f32[256,768]{1,0:T(8,128)S(1)}, f32[256,768]{1,0:T(8,128)}, u32[]{:S(2)}) copy-start(f32[256,768]{1,0:T(8,128)} %copy-done) | copy-start | bytes 2359300
  428.5 246.0 %copy-start.28 = (f32[768]{0:T(1024)S(1)}, f32[768]{0:T(1024)}, u32[]{:S(2)}) copy-start(f32[768]{0:T(1024)} %copy-done.27) | copy-start | bytes 9220
  428.5 246.0 %copy-start.30 = (f32[256]{0:T(256)S(1)}, f32[256]{0:T(256)}, u32[]{:S(2)}) copy-start(f32[256]{0:T(256)} %copy-done.29) | copy-start | bytes 3076
  428.5 247.6 %copy-start.18 = (bf16[256,12,64]{0,2,1:T(8,128)(2,1)S(1)}, bf16[256,12,64]{0,2,1:T(8,128)(2,1)}, u32[]{:S(2)}) copy-start(bf16[256,12,64]{0,2,1:T(8,128)(2,1)} %copy-done.17) | copy-start | bytes 1179652
  428.5 254.2 %reduce-scatter.18.cloned.1.call-start = ((), (), s32[]{:S(2)}) async-start(), calls=%async_computation.16 | async-start | bytes 221184
  432.2 334.4 %all-reduce.19.cloned.1.call-start = ((), (), s32[]{:S(2)}) async-start(), calls=%async_computation.17 | async-start | bytes 3833856 | tf_op jit(solution)/shard_map/psum | solution.py:343
  (37 other events, 159.7 us)
Sparse Core Ops, SparseCore 0:
  9.9 36.5 all-gather.10
  50.7 32.3 all-gather.12
  85.6 32.1 all-gather.14
  119.5 23.9 all-gather.16
  145.2 38.7 all-gather.18
  185.8 38.7 all-gather.20
  239.7 45.7 all-gather.22
  414.2 76.4 reduce-scatter.15
  494.4 36.6 reduce-scatter.9
  534.5 53.7 reduce-scatter.11
  591.7 53.7 reduce-scatter.13
  649.0 33.6 reduce-scatter.17
  685.9 80.6 all-reduce.18
